TPU v7x, 32 devices: a whole 2x2x4 slice. The times are simulated.
32 devices in a mesh: tx: 4 (over z), cell: 8 (over y, x, core).
Axes of the slice: x: 2, y: 2, z: 4, core: 2. Of those that a mesh axis runs over, the one named last changes fastest.
Arguments:
- currents: bfloat16 [2, 2, 8192, 4096], P(None, None, 'cell', 'tx'), may hold values from -6 to 6
- green: bfloat16 [2, 2, 64, 8192], P(None, None, 'tx', 'cell'), may hold values from -0.0625 to 0.0625
- angular_freq: float32 [2], replicated, may hold values from 0.5 to 3
- gate_time: float32 [64], replicated, may hold values from 0.1 to 3
Outputs:
- gated: float32 [64, 64, 4096], P(None, 'cell', 'tx')
All inputs are finite; a program needn't handle non-finite values.
Results may differ from a plain program's by a relative error of at most 0.0003.
Values may be sent and summed in bfloat16 or wider, within the bound.
No kernel may reach another device: no remote copies, remote signals or barrier semaphores. Data moves between devices by JAX's collectives and lax.ppermute only.
A program may use at most 128 MiB of HBM per device.

v0:
```python
import jax
import jax.numpy as jnp
from jax import lax
from jax.sharding import PartitionSpec as P


def complex_rows(green_block, currents):
    real_list = []
    imag_list = []
    for which_freq in range(currents.shape[1]):
        green_real = green_block[0, which_freq]
        green_imag = green_block[1, which_freq]
        curr_real = currents[0, which_freq]
        curr_imag = currents[1, which_freq]
        real_list.append(
            jnp.dot(green_real, curr_real, preferred_element_type=jnp.float32)
            - jnp.dot(green_imag, curr_imag, preferred_element_type=jnp.float32)
        )
        imag_list.append(
            jnp.dot(green_real, curr_imag, preferred_element_type=jnp.float32)
            + jnp.dot(green_imag, curr_real, preferred_element_type=jnp.float32)
        )
    return jnp.stack([jnp.stack(real_list), jnp.stack(imag_list)])


def per_device(currents, green, angular_freq, gate_time):
    gate_phase = gate_time[:, None] * angular_freq[None, :]
    cosine_weight = jnp.cos(gate_phase)
    sine_weight = jnp.sin(gate_phase)
    all_green = lax.all_gather(green, "tx", axis=2, tiled=True)
    receiver_portions = lax.psum_scatter(
        jnp.moveaxis(complex_rows(all_green, currents), 2, 0),
        "cell",
        scatter_dimension=0,
        tiled=True,
    )
    gated = jnp.einsum(
        "qc,ncm->qnm", cosine_weight, receiver_portions[:, 0], precision=lax.Precision.HIGHEST
    )
    gated = gated - jnp.einsum(
        "qc,ncm->qnm", sine_weight, receiver_portions[:, 1], precision=lax.Precision.HIGHEST
    )
    return gated


def solution(mesh):
    return jax.shard_map(
        per_device,
        mesh=mesh,
        in_specs=(P(None, None, "cell", "tx"), P(None, None, "tx", "cell"), P(), P()),
        out_specs=P(None, "cell", "tx"),
        check_vma=False,
    )
```

profile of v0, /device:TPU:0, one launch (start us, length us, event | category | flops | bytes accessed | tf_op | source)
XLA Modules:
  0.0 88.4 jit_solution(19578362142502962)
XLA Ops:
  6.5 0.0 reduce-scatter.2.cloned.1.call-start
  6.5 17.6 %all_gather.3 = bf16[2,2,64,1024]{3,2,1,0:T(8,128)(2,1)S(1)} all-gather(bf16[2,2,16,1024]{3,2,1,0:T(8,128)(2,1)} %param.5), channel_id=1, replica_groups=mesh['tx'=4,'cell'=8] {'tx'}, dimensions={2}, use_global_device_ids=true | all-gather | bytes 655360 | tf_op jit(solution)/shard_map/all_gather | solution.py:30
  24.1 0.0 copy-start
  24.1 2.2 %fusion = f32[64,1024]{1,0:T(8,128)S(1)} fusion(bf16[2,2,1024,1024]{3,2,1,0:T(8,128)(2,1)} %param.4, bf16[2,2,64,1024]{3,2,1,0:T(8,128)(2,1)S(1)} %all_gather.3), kind=kOutput, calls=%fused_computation | convolution fusion | flops 134217728 | bytes 2490368 | tf_op jit(solution)/shard_map/dot_general | solution.py:20
  26.3 2.5 %fusion.8 = f32[64,1024]{1,0:T(8,128)S(1)} fusion(bf16[2,2,1024,1024]{3,2,1,0:T(8,128)(2,1)} %param.4, bf16[2,2,64,1024]{3,2,1,0:T(8,128)(2,1)S(1)} %all_gather.3), kind=kOutput, calls=%fused_computation.8 | convolution fusion | flops 134217728 | bytes 2490368 | tf_op jit(solution)/shard_map/dot_general | solution.py:20
  28.8 2.1 %fusion.2 = f32[64,1024]{1,0:T(8,128)S(1)} fusion(bf16[2,2,1024,1024]{3,2,1,0:T(8,128)(2,1)} %param.4, bf16[2,2,64,1024]{3,2,1,0:T(8,128)(2,1)S(1)} %all_gather.3), kind=kOutput, calls=%fused_computation.2 | convolution fusion | flops 134217728 | bytes 2490368 | tf_op jit(solution)/shard_map/dot_general | solution.py:17
  30.9 2.1 %fusion.10 = f32[64,1024]{1,0:T(8,128)S(1)} fusion(bf16[2,2,1024,1024]{3,2,1,0:T(8,128)(2,1)} %param.4, bf16[2,2,64,1024]{3,2,1,0:T(8,128)(2,1)S(1)} %all_gather.3), kind=kOutput, calls=%fused_computation.10 | convolution fusion | flops 134217728 | bytes 2490368 | tf_op jit(solution)/shard_map/dot_general | solution.py:17
  33.0 0.0 copy-done
  33.0 0.5 fusion.45
  33.5 0.5 fusion.33
  34.0 0.5 fusion.39
  34.5 0.5 fusion.27
  35.0 0.1 maximum_bitcast_fusion.1
  35.0 0.0 copy-start.1
  35.0 0.0 copy-start.2
  35.1 1.1 %maximum_bitcast_fusion = f32[64,2,2,1024]{3,0,2,1:T(8,128)} fusion(f32[1,2,64,1024]{3,2,1,0:T(8,128)S(1)} %get-tuple-element.8, f32[1,2,64,1024]{3,2,1,0:T(8,128)S(1)} %get-tuple-element.7), kind=kLoop, calls=%fused_computation.33 | loop fusion | flops 262144 | bytes 2097152 | tf_op jit(solution)/shard_map/transpose | solution.py:32
  36.1 0.0 reduce-scatter.2.cloned.1.call-update
  36.2 38.0 %reduce-scatter.2.cloned.1.call-done = f32[8,2,2,1024]{3,0,2,1:T(8,128)} async-done(((f32[64,2,2,1024]{3,0,2,1:T(8,128)}), f32[8,2,2,1024]{3,0,2,1:T(8,128)}) %reduce-scatter.2.cloned.1.call-update) | async-done | bytes 131088 | tf_op jit(solution)/shard_map/reduce_scatter | solution.py:31
  74.1 0.9 slice_bitcast_fusion.12
  75.0 0.0 copy-done.1
  75.0 0.0 copy-done.2
  75.0 2.0 %fusion.49 = f32[64,8,1024]{2,0,1:T(8,128)S(1)} fusion(f32[8,2,1024]{2,0,1:T(8,128)S(1)} %get-tuple-element.6, f32[64]{0:T(128)S(1)} %copy-done.1, f32[2]{0:T(128)S(1)} %copy-done.2), kind=kOutput, calls=%fused_computation.43 | convolution fusion | flops 12583040 | bytes 2162952 | tf_op jit(solution)/shard_map/qc,ncm->qnm/dot_general | solution.py:37
  77.0 2.0 %convolution_subtract_fusion = f32[64,8,1024]{2,0,1:T(8,128)S(1)} fusion(f32[64,8,1024]{2,0,1:T(8,128)S(1)} %fusion.49, f32[8,2,1024]{2,0,1:T(8,128)S(1)} %get-tuple-element.5, f32[64]{0:T(128)S(1)} %copy-done.1, f32[2]{0:T(128)S(1)} %copy-done.2), kind=kOutput, calls=%fused_computation.24 | convolution fusion | flops 13107328 | bytes 4260104 | tf_op jit(solution)/shard_map/qc,ncm->qnm/dot_general | solution.py:40
  79.0 2.5 %copy.7 = f32[64,8,1024]{2,1,0:T(8,128)} copy(f32[64,8,1024]{2,0,1:T(8,128)S(1)} %convolution_subtract_fusion) | data formatting | bytes 4194304 | tf_op jit(solution)/shard_map/sub | solution.py:40
Async XLA Ops:
  6.5 67.6 %reduce-scatter.2.cloned.1.call-start = ((), (), s32[]{:S(2)}) async-start(), calls=%async_computation.1 | async-start | bytes 1179648 | tf_op jit(solution)/shard_map/reduce_scatter | solution.py:31
  24.1 8.9 %copy-start = (bf16[2,2,1024,1024]{3,2,1,0:T(8,128)(2,1)S(1)}, bf16[2,2,1024,1024]{3,2,1,0:T(8,128)(2,1)}, u32[]{:S(2)}) copy-start(bf16[2,2,1024,1024]{3,2,1,0:T(8,128)(2,1)} %param.4) | copy-start | bytes 25165828
  35.0 40.0 %copy-start.1 = (f32[64]{0:T(128)S(1)}, f32[64]{0:T(128)}, u32[]{:S(2)}) copy-start(f32[64]{0:T(128)} %param.7) | copy-start | bytes 772
  35.0 40.0 %copy-start.2 = (f32[2]{0:T(128)S(1)}, f32[2]{0:T(128)}, u32[]{:S(2)}) copy-start(f32[2]{0:T(128)} %param.6) | copy-start | bytes 28
Sparse Core Ops, SparseCore 0:
  36.3 37.7 reduce-scatter.1
where the time goes:
time: 88.6 us; the launch traced here: 88.4 us
  waiting for transfers between devices  38 us (43%)
  blocking collectives  17.6 us (20%)
  matrix products  14.8 us (17%)
  between operations  13.5 us (15%)
  local copies, waits for them, and re-layouts  3.43 us (4%)
  other arithmetic  1.16 us (1%)
    reduce_scatter x1, waiting for transfers between devices, per_device(): lax.psum_scatter(jnp.moveaxis(complex_rows(all_green, currents), 2, 0), '...  38 us
    all_gather x1, blocking collectives, per_device(): all_green = lax.all_gather(green, 'tx', axis=2, tiled=True)  17.6 us
    dot_general x2, matrix products, complex_rows(): jnp.dot(green_real, curr_imag, preferred_element_type=jnp.float32)  4.73 us
    dot_general x2, matrix products, complex_rows(): jnp.dot(green_imag, curr_imag, preferred_element_type=jnp.float32)  4.14 us
    sub x1, local copies, waits for them, and re-layouts, per_device(): gated - jnp.einsum('qc,ncm->qnm', sine_weight, receiver_portions[:, 1], p...  2.54 us
    dot_general x1, matrix products, per_device(): jnp.einsum('qc,ncm->qnm', sine_weight, receiver_portions[:, 1], precision...  2.02 us
    dot_general x1, matrix products, per_device(): jnp.einsum('qc,ncm->qnm', cosine_weight, receiver_portions[:, 0], precisi...  1.96 us
  transfers between devices with their start and end apart: 1, of which 1 were waited for; matrix products, arithmetic and copies ran while one was open for 0% of the time, Pallas kernels for 0%

commit v1 on v0

--- a/solution.py
+++ b/solution.py
@@ -27,7 +27,21 @@
     gate_phase = gate_time[:, None] * angular_freq[None, :]
     cosine_weight = jnp.cos(gate_phase)
     sine_weight = jnp.sin(gate_phase)
-    all_green = lax.all_gather(green, "tx", axis=2, tiled=True)
+    ways, here, step = (lax.axis_size("tx"), lax.axis_index("tx"), green.shape[2])
+    shape = [n * ways if d == 2 else n for d, n in enumerate(green.shape)]
+    full = lax.dynamic_update_slice_in_dim(
+        jnp.zeros(shape, green.dtype), green, here * step, axis=2
+    )
+    going_up = going_down = green
+    for far in range(1, ways // 2 + 1):
+        going_up = lax.ppermute(going_up, "tx", [(d, (d + 1) % ways) for d in range(ways)])
+        full = lax.dynamic_update_slice_in_dim(full, going_up, (here - far) % ways * step, axis=2)
+        if 2 * far < ways:
+            going_down = lax.ppermute(going_down, "tx", [(d, (d - 1) % ways) for d in range(ways)])
+            full = lax.dynamic_update_slice_in_dim(
+                full, going_down, (here + far) % ways * step, axis=2
+            )
+    all_green = full
     receiver_portions = lax.psum_scatter(
         jnp.moveaxis(complex_rows(all_green, currents), 2, 0),
         "cell",

time: 88.6 us -> 82.9 us (0.936)
  blocking collectives: 17.6 us -> 0 us
  waiting for transfers between devices: 38 us -> 45.8 us
  starting transfers between devices: 0.01 us -> 5.06 us
  matrix products: 14.8 us -> 12.6 us
  local copies, waits for them, and re-layouts: 3.43 us -> 4.45 us
    all_gather x1 -> x0, blocking collectives: 17.6 us -> none  [per_device(): all_green = lax.all_gather(green, 'tx', axis=2, tiled=True)]
    ppermute x0 -> x3, waiting for transfers between devices: none -> 10.2 us  [the longest x2 8.83 us: per_device(): lax.ppermute(going_up, 'tx', [(d, (d + 1) % ways) for d in range(ways)])]
    ppermute x0 -> x3, starting transfers between devices: none -> 5.05 us  [the longest x2 3.03 us: per_device(): lax.ppermute(going_up, 'tx', [(d, (d + 1) % ways) for d in range(ways)])]
    dot_general x2, matrix products: 4.73 us -> 0.96 us  [complex_rows(): jnp.dot(green_real, curr_imag, preferred_element_type=jnp.float32)]
    dot_general x2, matrix products: 0.96 us -> 4.14 us  [complex_rows(): jnp.dot(green_imag, curr_real, preferred_element_type=jnp.float32)]
    reduce_scatter x1, waiting for transfers between devices: 38 us -> 35.5 us  [per_device(): lax.psum_scatter(jnp.moveaxis(complex_rows(all_green, currents), 2, 0), '...]
    dot_general x2, matrix products: 4.14 us -> 2.55 us  [complex_rows(): jnp.dot(green_imag, curr_imag, preferred_element_type=jnp.float32)]
    dynamic_update_slice x0 -> x4, local copies, waits for them, and re-layouts: none -> 0.96 us  [the longest x1 0.93 us: per_device(): lax.dynamic_update_slice_in_dim(jnp.zeros(shape, green.dtype), green, her...]
  transfers between devices with their start and end apart: 1 -> 4, of which waited for: 1 -> 4; matrix products, arithmetic and copies ran while one was open for 0% -> 1% of each run, Pallas kernels for 0% -> 0%
where the time goes in v1:
time: 82.9 us; the launch traced here: 82.6 us
  waiting for transfers between devices  45.8 us (55%)
  between operations  13.6 us (16%)
  matrix products  12.6 us (15%)
  starting transfers between devices  5.06 us (6%)
  local copies, waits for them, and re-layouts  4.45 us (5%)
  other arithmetic  1.16 us (1%)
    reduce_scatter x1, waiting for transfers between devices, per_device(): lax.psum_scatter(jnp.moveaxis(complex_rows(all_green, currents), 2, 0), '...  35.5 us
    ppermute x2, waiting for transfers between devices, per_device(): lax.ppermute(going_up, 'tx', [(d, (d + 1) % ways) for d in range(ways)])  8.83 us
    dot_general x2, matrix products, complex_rows(): jnp.dot(green_imag, curr_real, preferred_element_type=jnp.float32)  4.14 us
    ppermute x2, starting transfers between devices, per_device(): lax.ppermute(going_up, 'tx', [(d, (d + 1) % ways) for d in range(ways)])  3.03 us
    dot_general x2, matrix products, complex_rows(): jnp.dot(green_imag, curr_imag, preferred_element_type=jnp.float32)  2.55 us
    sub x1, local copies, waits for them, and re-layouts, per_device(): gated - jnp.einsum('qc,ncm->qnm', sine_weight, receiver_portions[:, 1], p...  2.54 us
    ppermute x1, starting transfers between devices, per_device(): lax.ppermute(going_down, 'tx', [(d, (d - 1) % ways) for d in range(ways)])  2.03 us
    dot_general x1, matrix products, per_device(): jnp.einsum('qc,ncm->qnm', sine_weight, receiver_portions[:, 1], precision...  2.03 us
  transfers between devices with their start and end apart: 4, of which 4 were waited for; matrix products, arithmetic and copies ran while one was open for 1% of the time, Pallas kernels for 0%

profile of v1, /device:TPU:0, one launch (start us, length us, event | category | flops | bytes accessed | tf_op | source)
XLA Modules:
  0.0 82.6 jit_solution(12294898182432922167)
XLA Ops:
  6.5 0.0 reduce-scatter.2.cloned.1.call-start
  6.5 3.0 %collective-permute-start = (bf16[2,2,16,1024]{3,2,1,0:T(8,128)(2,1)}, bf16[2,2,16,1024]{3,2,1,0:T(8,128)(2,1)S(1)}, u32[]{:S(2)}, u32[]{:S(2)}) collective-permute-start(bf16[2,2,16,1024]{3,2,1,0:T(8,128)(2,1)} %param.5), channel_id=1, source_target_pairs={{0,8},{8,16},{16,24},{24,0},{1,9},{9,17},{17,25},{25,1},{2,10},{10... | collective-permute-start | bytes 393224 | tf_op jit(solution)/shard_map/ppermute | solution.py:37
  9.6 2.0 %collective-permute-start.1 = (bf16[2,2,16,1024]{3,2,1,0:T(8,128)(2,1)}, bf16[2,2,16,1024]{3,2,1,0:T(8,128)(2,1)S(1)}, u32[]{:S(2)}, u32[]{:S(2)}) collective-permute-start(bf16[2,2,16,1024]{3,2,1,0:T(8,128)(2,1)} %param.5), channel_id=1, source_target_pairs={{0,24},{8,0},{16,8},{24,16},{1,25},{9,1},{17,9},{25,17},{2,26},{10... | collective-permute-start | bytes 393224 | tf_op jit(solution)/shard_map/ppermute | solution.py:40
  11.6 0.1 broadcast_in_dim.2
  11.6 0.9 %constant_dynamic-update-slice_fusion.3 = bf16[2,2,64,1024]{3,2,1,0:T(8,128)(2,1)S(1)} fusion(bf16[2,2,64,1024]{3,2,1,0:T(8,128)(2,1)S(1)} %broadcast_in_dim.2, bf16[2,2,16,1024]{3,2,1,0:T(8,128)(2,1)} %param.5, s32[]{:T(128)S(6)} %select_n.27), kind=kLoop, calls=%fused_computation.52 | loop fusion | bytes 262148 | tf_op jit(solution)/shard_map/dynamic_update_slice | solution.py:32
  12.6 3.5 %collective-permute-done = bf16[2,2,16,1024]{3,2,1,0:T(8,128)(2,1)S(1)} collective-permute-done((bf16[2,2,16,1024]{3,2,1,0:T(8,128)(2,1)}, bf16[2,2,16,1024]{3,2,1,0:T(8,128)(2,1)S(1)}, u32[]{:S(2)}, u32[]{:S(2)}) %collective-permute-start) | collective-permute-done | bytes 131104 | tf_op jit(solution)/shard_map/ppermute | solution.py:37
  16.1 0.0 collective-permute-start.2
  16.1 0.0 copy-start
  16.2 1.4 %collective-permute-done.1 = bf16[2,2,16,1024]{3,2,1,0:T(8,128)(2,1)S(1)} collective-permute-done((bf16[2,2,16,1024]{3,2,1,0:T(8,128)(2,1)}, bf16[2,2,16,1024]{3,2,1,0:T(8,128)(2,1)S(1)}, u32[]{:S(2)}, u32[]{:S(2)}) %collective-permute-start.1) | collective-permute-done | bytes 131104 | tf_op jit(solution)/shard_map/ppermute | solution.py:40
  17.6 5.3 %collective-permute-done.2 = bf16[2,2,16,1024]{3,2,1,0:T(8,128)(2,1)S(1)} collective-permute-done((bf16[2,2,16,1024]{3,2,1,0:T(8,128)(2,1)S(1)}, bf16[2,2,16,1024]{3,2,1,0:T(8,128)(2,1)S(1)}, u32[]{:S(2)}, u32[]{:S(2)}) %collective-permute-start.2) | collective-permute-done | bytes 131104 | tf_op jit(solution)/shard_map/ppermute | solution.py:37
  22.9 2.1 %fusion.4 = f32[64,1024]{1,0:T(8,128)S(1)} fusion(bf16[2,2,1024,1024]{3,2,1,0:T(8,128)(2,1)} %param.4, bf16[2,2,64,1024]{3,2,1,0:T(8,128)(2,1)S(1)} %constant_dynamic-update-slice_fusion), kind=kOutput, calls=%fused_computation.4 | convolution fusion | flops 134217728 | bytes 2490368 | tf_op jit(solution)/shard_map/dot_general | solution.py:21
  25.0 2.1 %fusion.12 = f32[64,1024]{1,0:T(8,128)S(1)} fusion(bf16[2,2,1024,1024]{3,2,1,0:T(8,128)(2,1)} %param.4, bf16[2,2,64,1024]{3,2,1,0:T(8,128)(2,1)S(1)} %constant_dynamic-update-slice_fusion), kind=kOutput, calls=%fused_computation.12 | convolution fusion | flops 134217728 | bytes 2490368 | tf_op jit(solution)/shard_map/dot_general | solution.py:21
  27.1 2.1 %fusion.2 = f32[64,1024]{1,0:T(8,128)S(1)} fusion(bf16[2,2,1024,1024]{3,2,1,0:T(8,128)(2,1)} %param.4, bf16[2,2,64,1024]{3,2,1,0:T(8,128)(2,1)S(1)} %constant_dynamic-update-slice_fusion), kind=kOutput, calls=%fused_computation.2 | convolution fusion | flops 134217728 | bytes 2490368 | tf_op jit(solution)/shard_map/dot_general | solution.py:17
  29.1 0.0 copy-done
  29.2 0.5 fusion.10
  29.6 0.5 fusion.45
  30.1 0.5 fusion.33
  30.6 0.5 fusion.39
  31.1 0.5 fusion.27
  31.6 0.1 maximum_bitcast_fusion.1
  31.7 0.0 copy-start.1
  31.7 0.0 copy-start.2
  31.7 1.1 %maximum_bitcast_fusion = f32[64,2,2,1024]{3,0,2,1:T(8,128)} fusion(f32[1,2,64,1024]{3,2,1,0:T(8,128)S(1)} %get-tuple-element.8, f32[1,2,64,1024]{3,2,1,0:T(8,128)S(1)} %get-tuple-element.7), kind=kLoop, calls=%fused_computation.33 | loop fusion | flops 262144 | bytes 2097152 | tf_op jit(solution)/shard_map/transpose | solution.py:46
  32.8 0.0 reduce-scatter.2.cloned.1.call-update
  32.8 35.5 %reduce-scatter.2.cloned.1.call-done = f32[8,2,2,1024]{3,0,2,1:T(8,128)} async-done(((f32[64,2,2,1024]{3,0,2,1:T(8,128)}), f32[8,2,2,1024]{3,0,2,1:T(8,128)}) %reduce-scatter.2.cloned.1.call-update) | async-done | bytes 131088 | tf_op jit(solution)/shard_map/reduce_scatter | solution.py:45
  68.3 0.9 %slice_bitcast_fusion.12 = (f32[8,2,1024]{2,0,1:T(8,128)S(1)}, f32[8,2,1024]{2,0,1:T(8,128)S(1)}) fusion(f32[8,2,2,1024]{3,0,2,1:T(8,128)} %reduce-scatter.2.cloned.1.call-done), kind=kLoop, calls=%fused_computation.40 | loop fusion | bytes 262144 | tf_op jit(solution)/shard_map/squeeze | solution.py:55
  69.2 0.0 copy-done.1
  69.2 0.0 copy-done.2
  69.2 2.0 %fusion.49 = f32[64,8,1024]{2,0,1:T(8,128)S(1)} fusion(f32[8,2,1024]{2,0,1:T(8,128)S(1)} %get-tuple-element.6, f32[64]{0:T(128)S(1)} %copy-done.1, f32[2]{0:T(128)S(1)} %copy-done.2), kind=kOutput, calls=%fused_computation.43 | convolution fusion | flops 12583040 | bytes 2162952 | tf_op jit(solution)/shard_map/qc,ncm->qnm/dot_general | solution.py:51
  71.2 2.0 %convolution_subtract_fusion = f32[64,8,1024]{2,0,1:T(8,128)S(1)} fusion(f32[64,8,1024]{2,0,1:T(8,128)S(1)} %fusion.49, f32[8,2,1024]{2,0,1:T(8,128)S(1)} %get-tuple-element.5, f32[64]{0:T(128)S(1)} %copy-done.1, f32[2]{0:T(128)S(1)} %copy-done.2), kind=kOutput, calls=%fused_computation.24 | convolution fusion | flops 13107328 | bytes 4260104 | tf_op jit(solution)/shard_map/qc,ncm->qnm/dot_general | solution.py:54
  73.3 2.5 %copy.7 = f32[64,8,1024]{2,1,0:T(8,128)} copy(f32[64,8,1024]{2,0,1:T(8,128)S(1)} %convolution_subtract_fusion) | data formatting | bytes 4194304 | tf_op jit(solution)/shard_map/sub | solution.py:54
  (3 shorter events, 0.0 us)
Async XLA Ops:
  6.5 61.8 %reduce-scatter.2.cloned.1.call-start = ((), (), s32[]{:S(2)}) async-start(), calls=%async_computation.1 | async-start | bytes 1179648 | tf_op jit(solution)/shard_map/reduce_scatter | solution.py:45
  6.5 9.6 %collective-permute-start = (bf16[2,2,16,1024]{3,2,1,0:T(8,128)(2,1)}, bf16[2,2,16,1024]{3,2,1,0:T(8,128)(2,1)S(1)}, u32[]{:S(2)}, u32[]{:S(2)}) collective-permute-start(bf16[2,2,16,1024]{3,2,1,0:T(8,128)(2,1)} %param.5), channel_id=1, source_target_pairs={{0,8},{8,16},{16,24},{24,0},{1,9},{9,17},{17,25},{25,1},{2,10},{10... | collective-permute-start | bytes 393224 | tf_op jit(solution)/shard_map/ppermute | solution.py:37
  9.6 8.0 %collective-permute-start.1 = (bf16[2,2,16,1024]{3,2,1,0:T(8,128)(2,1)}, bf16[2,2,16,1024]{3,2,1,0:T(8,128)(2,1)S(1)}, u32[]{:S(2)}, u32[]{:S(2)}) collective-permute-start(bf16[2,2,16,1024]{3,2,1,0:T(8,128)(2,1)} %param.5), channel_id=1, source_target_pairs={{0,24},{8,0},{16,8},{24,16},{1,25},{9,1},{17,9},{25,17},{2,26},{10... | collective-permute-start | bytes 393224 | tf_op jit(solution)/shard_map/ppermute | solution.py:40
  16.1 6.8 %collective-permute-start.2 = (bf16[2,2,16,1024]{3,2,1,0:T(8,128)(2,1)S(1)}, bf16[2,2,16,1024]{3,2,1,0:T(8,128)(2,1)S(1)}, u32[]{:S(2)}, u32[]{:S(2)}) collective-permute-start(bf16[2,2,16,1024]{3,2,1,0:T(8,128)(2,1)S(1)} %collective-permute-done), channel_id=1, source_target_pairs={{0,8},{8,16},{16,24},{24,0},{1,9},{9,17},{17,25},{25,1},{2,10},{10... | collective-permute-start | bytes 393224 | tf_op jit(solution)/shard_map/ppermute | solution.py:37
  16.1 13.0 %copy-start = (bf16[2,2,1024,1024]{3,2,1,0:T(8,128)(2,1)S(1)}, bf16[2,2,1024,1024]{3,2,1,0:T(8,128)(2,1)}, u32[]{:S(2)}) copy-start(bf16[2,2,1024,1024]{3,2,1,0:T(8,128)(2,1)} %param.4) | copy-start | bytes 25165828
  31.7 37.6 %copy-start.1 = (f32[64]{0:T(128)S(1)}, f32[64]{0:T(128)}, u32[]{:S(2)}) copy-start(f32[64]{0:T(128)} %param.7) | copy-start | bytes 772
  31.7 37.6 %copy-start.2 = (f32[2]{0:T(128)S(1)}, f32[2]{0:T(128)}, u32[]{:S(2)}) copy-start(f32[2]{0:T(128)} %param.6) | copy-start | bytes 28
Sparse Core Ops, SparseCore 0:
  32.9 35.3 reduce-scatter.1
